TPU v7x, 128 devices: a whole 4x4x4 slice. The times are simulated.
128 devices in a mesh: pts: 32 (over x, y, core), grp: 4 (over z).
Axes of the slice: x: 4, y: 4, z: 4, core: 2. Of those that a mesh axis runs over, the one named last changes fastest.
Arguments:
- points: bfloat16 [262144, 256], P(('pts', 'grp')), may hold values from -6 to 6
- cotangent: bfloat16 [262144, 256], P(('pts', 'grp')), may hold values from -24 to 24
- gain_one: float32 [256], replicated, may hold values from 0.25 to 1.75
- gain_two: float32 [256], replicated, may hold values from 0.25 to 1.75
- w_mid: bfloat16 [256, 256], replicated, may hold values from -0.375 to 0.375
- w_feat: bfloat16 [256, 256], replicated, may hold values from -0.375 to 0.375
- w_out: bfloat16 [256, 256], replicated, may hold values from -0.375 to 0.375
- w_up: bfloat16 [256, 1024], replicated, may hold values from -0.375 to 0.375
- w_down: bfloat16 [256, 1024], replicated, may hold values from -0.1875 to 0.1875
- w_slice: float32 [32, 32], replicated, as said below
- w_temp: float32 [32], replicated, may hold values from -2 to 2
- query_matrix: float32 [32, 32], replicated
- key_matrix: float32 [32, 32], replicated
- value_matrix: float32 [32, 32], replicated, may hold values from -1 to 1
Outputs:
- grad_points: bfloat16 [262144, 256], P(('pts', 'grp'))
- grad_mid: float32 [256, 256], replicated
- grad_feat: float32 [256, 256], replicated
- grad_out: float32 [256, 256], replicated
- grad_up: float32 [256, 1024], replicated
- grad_down: float32 [256, 1024], replicated
- grad_gain_one: float32 [256], replicated
- grad_gain_two: float32 [256], replicated
- grad_slice: float32 [32, 32], replicated
- grad_temp: float32 [32], replicated
- grad_query: float32 [32, 32], replicated
- grad_key: float32 [32, 32], replicated
- grad_value: float32 [32, 32], replicated
Inputs may be any that keep to these rules, and one draw needn't show every extreme that they name: w_slice is a real matrix.
All inputs are finite; a program needn't handle non-finite values.
Results may differ from a plain program's by a relative error of at most 0.023.
The roundings to bfloat16 on the way count: a program that leaves them out, or rounds other values in their place, can miss the bound.
Values sent between devices are 32-bit elements; how exact they have to be, the bound alone decides.
A program may use at most 128 MiB of HBM per device.

v0:
```python
import jax
import jax.numpy as jnp
from jax import lax
from jax.sharding import PartitionSpec as P

HEADS = 8
HEAD_DIM = 32
EPS_NORM = 1e-05
EPS_SLICE = 1e-05
PRECISION_LEVEL = lax.Precision.HIGHEST


def layer_norm(value_rows, gain):
    centred = value_rows - jnp.mean(value_rows, axis=-1, keepdims=True)
    spread_tokens = jnp.mean(centred * centred, axis=-1, keepdims=True)
    return centred * lax.rsqrt(spread_tokens + EPS_NORM) * gain


def assign(middle, w_slice, w_temp):
    temper = 0.5 + jax.nn.softplus(
        jnp.einsum("nhd,d->nh", middle, w_temp, precision=PRECISION_LEVEL)
    )
    logits = (
        jnp.einsum("nhd,dm->nhm", middle, w_slice, precision=PRECISION_LEVEL) / temper[:, :, None]
    )
    return jax.nn.softmax(logits, axis=-1)


def mix_tokens(numerator_sums, denom, query_matrix, key_matrix, value_matrix):
    slice_token_rows = numerator_sums / (denom[:, :, None] + EPS_SLICE)
    query_rows = jnp.einsum(
        "xsf,fz->xsz", slice_token_rows, query_matrix, precision=PRECISION_LEVEL
    )
    key_rows = jnp.einsum("xsf,fz->xsz", slice_token_rows, key_matrix, precision=PRECISION_LEVEL)
    value_rows = jnp.einsum(
        "xsf,fz->xsz", slice_token_rows, value_matrix, precision=PRECISION_LEVEL
    )
    scores = jnp.einsum(
        "hme,hne->hmn", query_rows, key_rows, precision=PRECISION_LEVEL
    ) * slice_token_rows.shape[-1] ** (-0.5)
    probs = jax.nn.softmax(scores, axis=-1)
    return jnp.einsum("hmn,hne->hme", probs, value_rows, precision=PRECISION_LEVEL)


def transposed(left, right):
    return lax.dot_general(
        left, right, (((0,), (0,)), ((), ())), preferred_element_type=jnp.float32
    )


def against(left, right):
    return lax.dot_general(
        left, right, (((1,), (1,)), ((), ())), preferred_element_type=jnp.float32
    )


def local(
    points,
    cotangent,
    gain_one,
    gain_two,
    w_mid,
    w_feat,
    w_out,
    w_up,
    w_down,
    w_slice,
    w_temp,
    query_matrix,
    key_matrix,
    value_matrix,
):
    rows = points.shape[0]
    width = w_mid.shape[0]
    hidden_units = w_up.shape[1]
    points_f = points.astype(jnp.float32)
    normed = layer_norm(points_f, gain_one).astype(jnp.bfloat16)
    middle = jnp.dot(normed, w_mid, preferred_element_type=jnp.float32).astype(jnp.bfloat16)
    feats = jnp.dot(normed, w_feat, preferred_element_type=jnp.float32).astype(jnp.bfloat16)
    middle_f = middle.astype(jnp.float32).reshape(rows, HEADS, HEAD_DIM)
    weights = assign(middle_f, w_slice, w_temp)
    weight_rows_low = weights.astype(jnp.bfloat16)
    feature_rows_three = feats.reshape(rows, HEADS, HEAD_DIM)
    numerator_sums = jnp.einsum(
        "gux,guj->uxj", weight_rows_low, feature_rows_three, preferred_element_type=jnp.float32
    )
    denom = jnp.sum(weights, axis=0)
    numerator_sums, denom = lax.psum((numerator_sums, denom), ("pts", "grp"))
    mixed_token_low = mix_tokens(
        numerator_sums, denom, query_matrix, key_matrix, value_matrix
    ).astype(jnp.bfloat16)
    spread_tokens = jnp.einsum(
        "lge,gex->lgx", weight_rows_low, mixed_token_low, preferred_element_type=jnp.float32
    )
    spread_tokens = spread_tokens.astype(jnp.bfloat16).reshape(rows, width)
    resid = (points_f + jnp.dot(spread_tokens, w_out, preferred_element_type=jnp.float32)).astype(
        jnp.bfloat16
    )
    resid_f = resid.astype(jnp.float32)
    normed_two = layer_norm(resid_f, gain_two).astype(jnp.bfloat16)
    pre = jnp.dot(normed_two, w_up, preferred_element_type=jnp.float32)
    hidden = jax.nn.gelu(pre).astype(jnp.bfloat16)
    d_hid = jnp.dot(cotangent, w_down, preferred_element_type=jnp.float32)
    gelu_back = jax.vjp(jax.nn.gelu, pre)[1]
    d_pre = gelu_back(d_hid)[0].astype(jnp.bfloat16)
    d_norm_two = against(d_pre, w_up)
    norm_back_two = jax.vjp(layer_norm, resid_f, gain_two)[1]
    d_res_ln, d_gain_two = norm_back_two(d_norm_two)
    d_resid = cotangent.astype(jnp.float32) + d_res_ln
    d_resid_b = d_resid.astype(jnp.bfloat16)
    spread_gradient = against(d_resid_b, w_out).astype(jnp.bfloat16).reshape(rows, HEADS, HEAD_DIM)
    mixed_gradient = jnp.einsum(
        "gux,guj->uxj", weight_rows_low, spread_gradient, preferred_element_type=jnp.float32
    )
    mixed_gradient = lax.psum(mixed_gradient, ("pts", "grp"))
    token_back = jax.vjp(mix_tokens, numerator_sums, denom, query_matrix, key_matrix, value_matrix)[
        1
    ]
    numerator_gradient, denominator_gradient, grad_query, grad_key, grad_value = token_back(
        mixed_gradient
    )
    weight_gradient = jnp.einsum(
        "wkt,klt->wkl", spread_gradient, mixed_token_low, preferred_element_type=jnp.float32
    )
    weight_gradient = (
        weight_gradient
        + jnp.einsum("wkt,klt->wkl", feature_rows_three.astype(jnp.float32), numerator_gradient)
        + denominator_gradient[None, :, :]
    )
    feature_gradient = jnp.einsum(
        "lge,gex->lgx", weight_rows_low.astype(jnp.float32), numerator_gradient
    )
    feature_gradient = feature_gradient.astype(jnp.bfloat16).reshape(rows, width)
    assign_back = jax.vjp(assign, middle_f, w_slice, w_temp)[1]
    d_mid, d_slice, d_temp = assign_back(weight_gradient)
    d_mid = d_mid.reshape(rows, width).astype(jnp.bfloat16)
    d_normed = against(d_mid, w_mid) + against(feature_gradient, w_feat)
    norm_back_one = jax.vjp(layer_norm, points_f, gain_one)[1]
    d_ln, d_gain_one = norm_back_one(d_normed)
    grad_points = (d_resid + d_ln).astype(jnp.bfloat16)

    def rows_of(left, right):
        return transposed(left, right)

    big = lax.psum(
        jnp.concatenate(
            [
                rows_of(normed, d_mid),
                rows_of(normed, feature_gradient),
                rows_of(spread_tokens, d_resid_b),
                rows_of(normed_two, d_pre),
                rows_of(cotangent, hidden),
            ],
            axis=1,
        ),
        ("pts", "grp"),
    )
    g_slice, g_temp, g_one, g_two = lax.psum(
        (d_slice, d_temp, d_gain_one, d_gain_two), ("pts", "grp")
    )
    return (
        grad_points,
        big[:, :width],
        big[:, width : 2 * width],
        big[:, 2 * width : 3 * width],
        big[:, 3 * width : 3 * width + hidden_units],
        big[:, 3 * width + hidden_units :],
        g_one,
        g_two,
        g_slice,
        g_temp,
        grad_query,
        grad_key,
        grad_value,
    )


def solution(mesh):
    return jax.shard_map(
        local,
        mesh=mesh,
        in_specs=(
            P(("pts", "grp"), None),
            P(("pts", "grp"), None),
            P(),
            P(),
            P(),
            P(),
            P(),
            P(),
            P(),
            P(),
            P(),
            P(),
            P(),
            P(),
        ),
        out_specs=(
            P(("pts", "grp"), None),
            P(),
            P(),
            P(),
            P(),
            P(),
            P(),
            P(),
            P(),
            P(),
            P(),
            P(),
            P(),
        ),
        check_vma=False,
    )
```

profile of v0, /device:TPU:1, one launch (start us, length us, event | category | flops | bytes accessed | tf_op | source)
XLA Modules:
  0.0 370.1 jit_solution(17323691424581522889)
XLA Ops:
  7.3 1.6 copy.28
  9.4 1.4 copy.27
  10.8 1.5 convolution_convert_fusion.3
  12.4 0.6 convolution_convert_fusion.4
  13.1 2.5 fusion.70
  15.5 6.6 %fusion.74 = f32[1,2048,8]{0,1,2:T(8,128)} fusion(bf16[2048,8,32]{0,2,1:T(8,128)(2,1)S(1)} %bitcast.132, f32[32]{0:T(128)S(1)} %copy-done.57), kind=kOutput, calls=%fused_computation.133 | convolution fusion | flops 6291456 | bytes 1114240 | tf_op jit(solution)/shard_map/nhd,d->nh/dot_general | solution.py:21
  22.1 5.2 %copy.46 = f32[1,2048,8]{1,2,0:T(8,128)S(1)} copy(f32[1,2048,8]{0,1,2:T(8,128)} %fusion.74) | data formatting | bytes 131072 | tf_op jit(solution)/shard_map/nhd,d->nh/dot_general | solution.py:21
  27.4 2.3 fusion.89
  30.1 1.6 copy-done.20
  32.2 70.0 %all-reduce.1 = (f32[8,32,32]{2,1,0:T(8,128)S(1)}, f32[8,32]{1,0:T(8,128)S(1)}) all-reduce(f32[8,32,32]{2,1,0:T(8,128)S(1)} %fusion.91, f32[8,32]{1,0:T(8,128)S(1)} %get-tuple-element.43), channel_id=1, replica_groups=mesh['pts'=32,'grp'=4] {'pts','grp'}, use_global_device_ids=true, to_apply=%region_4.5 | all-reduce | flops 8448 | bytes 67584 | tf_op jit(solution)/shard_map/psum | solution.py:88
  103.2 1.3 fusion.67
  105.8 0.5 convert_reduce_fusion.1
  106.8 1.4 fusion.43
  108.3 6.3 %fusion.7 = bf16[2048,1024]{1,0:T(8,128)(2,1)S(1)} fusion(f32[2048,1024]{1,0:T(8,128)S(1)} %fusion.43, bf16[2048,256]{1,0:T(8,128)(2,1)S(1)} %copy-done.27, bf16[256,1024]{1,0:T(8,128)(2,1)S(1)} %copy-done.59), kind=kOutput, calls=%fused_computation.9 | convolution fusion | flops 1115684864 | bytes 14155776 | tf_op jit(solution)/shard_map/dot_general | solution.py:103
  114.6 1.4 fusion.32
  116.0 0.6 copy-done.60
  116.5 2.0 fusion.30
  118.6 0.8 fusion.37
  119.9 0.5 copy-done.15
  120.4 1.0 copy-done.11
  121.8 63.1 %psum.58 = f32[8,32,32]{2,1,0:T(8,128)S(1)} all-reduce(f32[8,32,32]{2,1,0:T(8,128)S(1)} %fusion.93), channel_id=1, replica_groups=mesh['pts'=32,'grp'=4] {'pts','grp'}, use_global_device_ids=true, to_apply=%region_13.14 | all-reduce | flops 8192 | bytes 65536 | tf_op jit(solution)/shard_map/psum | solution.py:115
  185.2 1.3 multiply_reduce_fusion.3
  186.6 1.3 fusion.80
  187.9 1.3 fusion.81
  190.6 0.6 convolution_convert_fusion.1
  191.6 0.8 multiply_reduce_fusion.1
  192.4 1.1 copy-done.17
  193.6 1.0 multiply_reduce_fusion
  194.8 2.1 fusion.22
  196.9 1.4 convolution_dynamic-update-slice_fusion.3
  198.3 1.3 convolution_dynamic-update-slice_fusion.2
  200.2 1.2 convolution_dynamic-update-slice_fusion.1
  201.4 2.3 convolution_dynamic-update-slice_fusion
  203.8 4.3 %fusion.36 = f32[256,2816]{1,0:T(8,128)} fusion(f32[256,2816]{1,0:T(8,128)} %convolution_dynamic-update-slice_fusion, bf16[2048,256]{1,0:T(8,128)(2,1)S(1)} %copy-done.28, f32[2048,1024]{1,0:T(8,128)S(1)} %bitcast.126), kind=kOutput, calls=%fused_computation.60 | convolution fusion | flops 1092616192 | bytes 10485760 | tf_op jit(solution)/shard_map/dot_general | solution.py:46
  208.1 1.8 fusion.94
  209.9 0.7 fusion.34
  210.7 1.5 fusion.28
  212.5 2.5 add_convert_fusion
  215.0 2.3 copy.44
  217.3 1.0 convolution_bitcast_fusion.4
  218.3 2.9 convolution_bitcast_fusion.3
  221.3 64.4 %all-reduce = (f32[256]{0:T(256)}, f32[256]{0:T(256)}, f32[32,32]{1,0:T(8,128)}, f32[32]{0:T(128)}) all-reduce(f32[256]{0:T(256)S(1)} %get-tuple-element.28, f32[256]{0:T(256)S(1)} %copy-done.56, f32[32,32]{1,0:T(8,128)S(1)} %convolution_bitcast_fusion.3, ...), channel_id=1, replica_groups=mesh['pts'=32,'grp'=4] {'pts','grp'}, use_global_device_ids=true, to_apply=%region_22.23 | all-reduce | flops 1568 | bytes 12544 | tf_op jit(solution)/shard_map/psum | solution.py:158
  285.6 1.1 convolution_bitcast_fusion.1
  286.7 1.1 convolution_bitcast_fusion.2
  287.8 1.1 convolution_bitcast_fusion
  288.9 69.1 %all-reduce.4.cloned.1.call-done = f32[256,2816]{1,0:T(8,128)} async-done(((f32[256,2816]{1,0:T(8,128)}), f32[256,2816]{1,0:T(8,128)}) %all-reduce.4.cloned.1.call-update) | async-done | bytes 2883600 | tf_op jit(solution)/shard_map/psum | solution.py:145
  358.0 2.0 fusion.88
  360.0 3.1 fusion.87
  (160 shorter events, 8.2 us)
Async XLA Ops:
  7.2 99.6 %copy-start = (bf16[256,1024]{1,0:T(8,128)(2,1)S(1)}, bf16[256,1024]{1,0:T(8,128)(2,1)}, u32[]{:S(2)}) copy-start(bf16[256,1024]{1,0:T(8,128)(2,1)} %param.21) | copy-start | bytes 1572868
  7.2 2.2 copy-start.26
  7.2 350.8 %all-reduce.4.cloned.1.call-start = ((), (), s32[]{:S(2)}) async-start(), calls=%async_computation | async-start | bytes 5767168 | tf_op jit(solution)/shard_map/psum | solution.py:145
  8.9 2.0 copy-start.31
  8.9 2.0 copy-start.54
  9.4 3.0 copy-start.30
  12.9 9.2 %copy-start.18 = (bf16[2048,256]{0,1:T(8,128)(2,1)}, bf16[2048,256]{0,1:T(8,128)(2,1)S(1)}, u32[]{:S(2)}) copy-start(bf16[2048,256]{0,1:T(8,128)(2,1)S(1)} %convolution_convert_fusion.4) | copy-start | bytes 3145732
  12.9 2.6 copy-start.57
  27.4 2.3 copy-start.43
  29.7 2.5 copy-start.6
  29.7 2.0 copy-start.20
  29.7 72.5 %copy-start.50 = (f32[32,32]{1,0:T(8,128)S(1)}, f32[32,32]{1,0:T(8,128)}, u32[]{:S(2)}) copy-start(f32[32,32]{1,0:T(8,128)} %param.26) | copy-start | bytes 12292
  30.1 75.2 %copy-start.1 = (bf16[2048,8,32]{0,2,1:T(8,128)(2,1)}, bf16[2048,8,32]{0,2,1:T(8,128)(2,1)S(1)}, u32[]{:S(2)}) copy-start(bf16[2048,8,32]{0,2,1:T(8,128)(2,1)S(1)} %get-tuple-element.44) | copy-start | bytes 3145732
  30.1 72.8 %copy-start.48 = (f32[32,32]{1,0:T(8,128)S(1)}, f32[32,32]{1,0:T(8,128)}, u32[]{:S(2)}) copy-start(f32[32,32]{1,0:T(8,128)} %param.27) | copy-start | bytes 12292
  30.1 73.1 %copy-start.52 = (f32[32,32]{1,0:T(8,128)S(1)}, f32[32,32]{1,0:T(8,128)}, u32[]{:S(2)}) copy-start(f32[32,32]{1,0:T(8,128)} %param.25) | copy-start | bytes 12292
  102.9 3.5 copy-start.33
  102.9 3.0 copy-start.29
  103.2 3.2 copy-start.42
  104.5 1.9 copy-start.34
  108.3 6.3 %copy-start.8 = (f32[2048,1024]{1,0:T(8,128)}, f32[2048,1024]{1,0:T(8,128)S(1)}, u32[]{:S(2)}) copy-start(f32[2048,1024]{1,0:T(8,128)S(1)} %fusion.43) | copy-start | bytes 25165828
  114.6 2.0 copy-start.60
  116.5 2.9 copy-start.4
  116.5 2.1 copy-start.13
  119.4 2.0 copy-start.2
  184.9 4.2 %copy-start.12 = (bf16[2048,256]{0,1:T(8,128)(2,1)S(1)}, bf16[2048,256]{0,1:T(8,128)(2,1)}, u32[]{:S(2)}) copy-start(bf16[2048,256]{0,1:T(8,128)(2,1)} %copy-done.11) | copy-start | bytes 3145732
  185.2 4.4 %copy-start.35 = (f32[8,32,32]{2,1,0:T(8,128)}, f32[8,32,32]{2,1,0:T(8,128)S(1)}, u32[]{:S(2)}) copy-start(f32[8,32,32]{2,1,0:T(8,128)S(1)} %fusion.56) | copy-start | bytes 98308
  186.5 3.1 copy-start.49
  187.9 2.3 copy-start.40
  187.9 2.0 copy-start.51
  189.6 1.9 copy-start.21
  191.6 6.7 %copy-start.22 = (bf16[8,32,2048]{2,1,0:T(8,128)(2,1)}, bf16[8,32,2048]{2,1,0:T(8,128)(2,1)S(1)}, u32[]{:S(2)}) copy-start(bf16[8,32,2048]{2,1,0:T(8,128)(2,1)S(1)} %convolution_convert_fusion.1) | copy-start | bytes 3145732
  191.6 2.0 copy-start.17
  194.6 2.2 copy-start.24
  194.7 2.2 copy-start.55
  194.7 6.7 %copy-start.61 = (bf16[2048,1024]{1,0:T(8,128)(2,1)S(1)}, bf16[2048,1024]{1,0:T(8,128)(2,1)}, u32[]{:S(2)}) copy-start(bf16[2048,1024]{1,0:T(8,128)(2,1)} %copy-done.60) | copy-start | bytes 12582916
  196.9 2.8 copy-start.25
  196.9 6.9 %slice-start = ((s8[8388608]{0:T(1024)(128)(4,1)}), s8[4194304]{0:T(1024)(128)(4,1)S(1)}, s32[]{:S(2)}) async-start(s8[8388608]{0:T(1024)(128)(4,1)} %bitcast.125), calls=%async_computation.1 | async-start | bytes 8388608
  198.3 1.9 copy-start.16
  200.2 3.6 slice-start.1
  201.4 2.3 copy-start.28
  208.1 1.8 copy-start.23
  208.1 1.8 copy-start.32
  210.7 1.8 copy-start.14
  215.0 2.4 copy-start.19
  218.3 2.9 copy-start.56
  218.3 67.3 %copy-start.39 = (f32[8,32,32]{2,1,0:T(8,128)S(1)}, f32[8,32,32]{2,1,0:T(8,128)}, u32[]{:S(2)}) copy-start(f32[8,32,32]{2,1,0:T(8,128)} %copy-done.37) | copy-start | bytes 98308
  218.3 68.4 %copy-start.41 = (f32[8,32,32]{2,1,0:T(8,128)S(1)}, f32[8,32,32]{2,1,0:T(8,128)}, u32[]{:S(2)}) copy-start(f32[8,32,32]{2,1,0:T(8,128)} %copy-done.40) | copy-start | bytes 98308
  218.3 69.5 %copy-start.36 = (f32[8,32,32]{2,1,0:T(8,128)S(1)}, f32[8,32,32]{2,1,0:T(8,128)}, u32[]{:S(2)}) copy-start(f32[8,32,32]{2,1,0:T(8,128)} %copy-done.35) | copy-start | bytes 98308
  (17 other events, 19.9 us)
Sparse Core Ops, SparseCore 0:
  208.2 149.6 all-reduce.3
where the time goes:
time: 376 us; the launch traced here: 370 us
  blocking collectives  197 us (52%)
  waiting for transfers between devices  69.1 us (18%)
  matrix products  54.2 us (14%)
  local copies, waits for them, and re-layouts  22.5 us (6%)
  between operations  15.2 us (4%)
  other arithmetic  11.5 us (3%)
    psum x1, blocking collectives, local(): numerator_sums, denom = lax.psum((numerator_sums, denom), ('pts', 'grp'))  70 us
    psum x1, waiting for transfers between devices, local(): lax.psum(jnp.concatenate([rows_of(normed, d_mid), rows_of(normed, feature...  69.1 us
    psum x1, blocking collectives, local(): lax.psum((d_slice, d_temp, d_gain_one, d_gain_two), ('pts', 'grp'))  64.4 us
    psum x1, blocking collectives, local(): mixed_gradient = lax.psum(mixed_gradient, ('pts', 'grp'))  63.1 us
    unnamed x131, local copies, waits for them, and re-layouts  12.2 us
    dot_general x5, matrix products, transposed(): lax.dot_general(left, right, (((0,), (0,)), ((), ())), preferred_element_...  10.6 us
  transfers between devices with their start and end apart: 1, of which 1 were waited for; matrix products, arithmetic and copies ran while one was open for 4% of the time, Pallas kernels for 0%

commit v1 on v0

--- a/solution.py
+++ b/solution.py
@@ -156,7 +156,7 @@
         ("pts", "grp"),
     )
     g_slice, g_temp, g_one, g_two = lax.psum(
-        (d_slice, d_temp, d_gain_one, d_gain_two), ("pts", "grp")
+        lax.psum((d_slice, d_temp, d_gain_one, d_gain_two), "grp"), "pts"
     )
     return (
         grad_points,

time: 376 us -> 383 us (1.019)
  the two profiles are of different devices: /device:TPU:1 before, /device:TPU:0 now
where the time goes in v1:
time: 383 us; the launch traced here: 377 us
  blocking collectives  273 us (71%)
  matrix products  54.3 us (14%)
  local copies, waits for them, and re-layouts  22.5 us (6%)
  between operations  15.2 us (4%)
  other arithmetic  11.5 us (3%)
    psum x1, blocking collectives, local(): lax.psum(lax.psum((d_slice, d_temp, d_gain_one, d_gain_two), 'grp'), 'pts')  124 us
    psum x1, blocking collectives, local(): numerator_sums, denom = lax.psum((numerator_sums, denom), ('pts', 'grp'))  69.5 us
    psum x1, blocking collectives, local(): mixed_gradient = lax.psum(mixed_gradient, ('pts', 'grp'))  62.8 us
    psum x1, blocking collectives, local(): lax.psum((d_slice, d_temp, d_gain_one, d_gain_two), 'grp')  16.8 us
    unnamed x129, local copies, waits for them, and re-layouts  12.2 us
    dot_general x5, matrix products, transposed(): lax.dot_general(left, right, (((0,), (0,)), ((), ())), preferred_element_...  10.7 us
  transfers between devices with their start and end apart: 1, of which 0 were waited for; matrix products, arithmetic and copies ran while one was open for 4% of the time, Pallas kernels for 0%

profile of v1, /device:TPU:0, one launch (start us, length us, event | category | flops | bytes accessed | tf_op | source)
XLA Modules:
  0.0 376.6 jit_solution(17413422152228989870)
XLA Ops:
  7.3 1.6 copy.28
  9.4 1.4 copy.27
  10.8 1.5 convolution_convert_fusion.3
  12.4 0.6 convolution_convert_fusion.4
  13.1 2.5 fusion.70
  15.5 6.5 %fusion.74 = f32[1,2048,8]{0,1,2:T(8,128)} fusion(bf16[2048,8,32]{0,2,1:T(8,128)(2,1)S(1)} %bitcast.132, f32[32]{0:T(128)S(1)} %copy-done.56), kind=kOutput, calls=%fused_computation.133 | convolution fusion | flops 6291456 | bytes 1114240 | tf_op jit(solution)/shard_map/nhd,d->nh/dot_general | solution.py:21
  22.1 5.2 %copy.46 = f32[1,2048,8]{1,2,0:T(8,128)S(1)} copy(f32[1,2048,8]{0,1,2:T(8,128)} %fusion.74) | data formatting | bytes 131072 | tf_op jit(solution)/shard_map/nhd,d->nh/dot_general | solution.py:21
  27.4 2.3 fusion.89
  30.1 1.6 copy-done.20
  32.2 69.5 %all-reduce = (f32[8,32,32]{2,1,0:T(8,128)S(1)}, f32[8,32]{1,0:T(8,128)S(1)}) all-reduce(f32[8,32,32]{2,1,0:T(8,128)S(1)} %fusion.91, f32[8,32]{1,0:T(8,128)S(1)} %get-tuple-element.47), channel_id=1, replica_groups=mesh['pts'=32,'grp'=4] {'pts','grp'}, use_global_device_ids=true, to_apply=%region_4.5 | all-reduce | flops 8448 | bytes 67584 | tf_op jit(solution)/shard_map/psum | solution.py:88
  102.7 1.3 fusion.67
  105.3 0.5 convert_reduce_fusion.1
  106.3 1.4 fusion.43
  107.8 6.3 %fusion.7 = bf16[2048,1024]{1,0:T(8,128)(2,1)S(1)} fusion(f32[2048,1024]{1,0:T(8,128)S(1)} %fusion.43, bf16[2048,256]{1,0:T(8,128)(2,1)S(1)} %copy-done.27, bf16[256,1024]{1,0:T(8,128)(2,1)S(1)} %copy-done.58), kind=kOutput, calls=%fused_computation.9 | convolution fusion | flops 1115684864 | bytes 14155776 | tf_op jit(solution)/shard_map/dot_general | solution.py:103
  114.1 1.4 fusion.32
  115.4 0.6 copy-done.59
  116.0 2.0 fusion.30
  118.1 0.8 fusion.37
  119.4 0.5 copy-done.15
  119.9 1.0 copy-done.11
  121.3 62.8 %psum.86 = f32[8,32,32]{2,1,0:T(8,128)S(1)} all-reduce(f32[8,32,32]{2,1,0:T(8,128)S(1)} %fusion.93), channel_id=1, replica_groups=mesh['pts'=32,'grp'=4] {'pts','grp'}, use_global_device_ids=true, to_apply=%region_13.14 | all-reduce | flops 8192 | bytes 65536 | tf_op jit(solution)/shard_map/psum | solution.py:115
  184.5 1.3 multiply_reduce_fusion.3
  185.8 1.3 fusion.80
  187.2 1.3 fusion.81
  189.9 0.6 convolution_convert_fusion.1
  190.9 0.8 multiply_reduce_fusion.1
  191.7 1.1 copy-done.17
  192.8 1.0 multiply_reduce_fusion
  194.0 2.1 fusion.22
  196.2 1.4 convolution_dynamic-update-slice_fusion.3
  197.6 1.4 convolution_dynamic-update-slice_fusion.2
  199.5 1.2 convolution_dynamic-update-slice_fusion.1
  200.7 2.3 convolution_dynamic-update-slice_fusion
  203.0 4.3 %fusion.36 = f32[256,2816]{1,0:T(8,128)} fusion(f32[256,2816]{1,0:T(8,128)} %convolution_dynamic-update-slice_fusion, bf16[2048,256]{1,0:T(8,128)(2,1)S(1)} %copy-done.28, f32[2048,1024]{1,0:T(8,128)S(1)} %bitcast.126), kind=kOutput, calls=%fused_computation.60 | convolution fusion | flops 1092616192 | bytes 10485760 | tf_op jit(solution)/shard_map/dot_general | solution.py:46
  207.4 1.8 fusion.94
  209.2 0.7 fusion.34
  210.0 1.5 fusion.28
  211.8 2.5 add_convert_fusion
  214.3 2.3 copy.44
  216.6 1.0 convolution_bitcast_fusion.4
  217.6 2.9 convolution_bitcast_fusion.3
  220.6 16.8 %all-reduce.2 = (f32[256]{0:T(256)S(1)}, f32[256]{0:T(256)S(1)}, f32[32,32]{1,0:T(8,128)S(1)}, f32[32]{0:T(128)S(1)}) all-reduce(f32[256]{0:T(256)S(1)} %get-tuple-element.28, f32[256]{0:T(256)S(1)} %copy-done.55, f32[32,32]{1,0:T(8,128)S(1)} %convolution_bitcast_fusion.3, ...), channel_id=1, replica_groups=mesh['pts'=32,'grp'=4] {'grp'}, use_global_device_ids=true, to_apply=%region_22.23 | all-reduce | flops 1568 | bytes 12544 | tf_op jit(solution)/shard_map/psum | solution.py:159
  237.4 123.8 %all-reduce.1 = (f32[256]{0:T(256)}, f32[256]{0:T(256)}, f32[32,32]{1,0:T(8,128)}, f32[32]{0:T(128)}) all-reduce(f32[256]{0:T(256)S(1)} %get-tuple-element.36, f32[256]{0:T(256)S(1)} %get-tuple-element.37, f32[32,32]{1,0:T(8,128)S(1)} %get-tuple-element.38, f32[32]{0:T(128)S(1)} %get-tuple-element.39), channel_id=1, replica_groups=mesh['pts'=32,'grp'=4] {'pts'}, use_global_device_ids=true, to_apply=%region_23.24 | all-reduce | flops 1568 | bytes 12544 | tf_op jit(solution)/shard_map/psum | solution.py:158
  361.2 1.1 convolution_bitcast_fusion.1
  362.3 1.1 convolution_bitcast_fusion.2
  363.4 1.1 convolution_bitcast_fusion
  364.5 2.0 fusion.88
  366.5 3.1 fusion.87
  (159 shorter events, 8.1 us)
Async XLA Ops:
  7.2 99.1 %copy-start = (bf16[256,1024]{1,0:T(8,128)(2,1)S(1)}, bf16[256,1024]{1,0:T(8,128)(2,1)}, u32[]{:S(2)}) copy-start(bf16[256,1024]{1,0:T(8,128)(2,1)} %param.21) | copy-start | bytes 1572868
  7.2 2.2 copy-start.26
  7.2 357.3 %all-reduce.5.cloned.1.call-start = ((), (), s32[]{:S(2)}) async-start(), calls=%async_computation | async-start | bytes 5767168 | tf_op jit(solution)/shard_map/psum | solution.py:145
  8.9 2.0 copy-start.31
  8.9 2.0 copy-start.53
  9.4 3.0 copy-start.30
  12.9 2.6 copy-start.18
  12.9 2.6 copy-start.56
  27.4 2.3 copy-start.42
  29.6 2.5 copy-start.6
  29.7 2.0 copy-start.20
  29.7 72.0 %copy-start.49 = (f32[32,32]{1,0:T(8,128)S(1)}, f32[32,32]{1,0:T(8,128)}, u32[]{:S(2)}) copy-start(f32[32,32]{1,0:T(8,128)} %param.26) | copy-start | bytes 12292
  30.0 74.8 %copy-start.1 = (bf16[2048,8,32]{0,2,1:T(8,128)(2,1)}, bf16[2048,8,32]{0,2,1:T(8,128)(2,1)S(1)}, u32[]{:S(2)}) copy-start(bf16[2048,8,32]{0,2,1:T(8,128)(2,1)S(1)} %get-tuple-element.48) | copy-start | bytes 3145732
  30.1 72.3 %copy-start.47 = (f32[32,32]{1,0:T(8,128)S(1)}, f32[32,32]{1,0:T(8,128)}, u32[]{:S(2)}) copy-start(f32[32,32]{1,0:T(8,128)} %param.27) | copy-start | bytes 12292
  30.1 72.6 %copy-start.51 = (f32[32,32]{1,0:T(8,128)S(1)}, f32[32,32]{1,0:T(8,128)}, u32[]{:S(2)}) copy-start(f32[32,32]{1,0:T(8,128)} %param.25) | copy-start | bytes 12292
  102.3 3.5 copy-start.33
  102.3 2.9 copy-start.29
  102.7 3.2 copy-start.41
  104.0 1.9 copy-start.34
  107.7 6.3 %copy-start.8 = (f32[2048,1024]{1,0:T(8,128)}, f32[2048,1024]{1,0:T(8,128)S(1)}, u32[]{:S(2)}) copy-start(f32[2048,1024]{1,0:T(8,128)S(1)} %fusion.43) | copy-start | bytes 25165828
  114.0 2.0 copy-start.59
  116.0 2.9 copy-start.4
  116.0 2.1 copy-start.13
  118.9 2.0 copy-start.2
  184.2 4.2 %copy-start.12 = (bf16[2048,256]{0,1:T(8,128)(2,1)S(1)}, bf16[2048,256]{0,1:T(8,128)(2,1)}, u32[]{:S(2)}) copy-start(bf16[2048,256]{0,1:T(8,128)(2,1)} %copy-done.11) | copy-start | bytes 3145732
  184.5 4.4 %copy-start.35 = (f32[8,32,32]{2,1,0:T(8,128)}, f32[8,32,32]{2,1,0:T(8,128)S(1)}, u32[]{:S(2)}) copy-start(f32[8,32,32]{2,1,0:T(8,128)S(1)} %fusion.56) | copy-start | bytes 98308
  185.8 3.1 copy-start.48
  187.1 2.3 copy-start.39
  187.1 2.0 copy-start.50
  188.9 1.7 copy-start.7
  188.9 1.9 copy-start.21
  190.9 6.7 %copy-start.22 = (bf16[8,32,2048]{2,1,0:T(8,128)(2,1)}, bf16[8,32,2048]{2,1,0:T(8,128)(2,1)S(1)}, u32[]{:S(2)}) copy-start(bf16[8,32,2048]{2,1,0:T(8,128)(2,1)S(1)} %convolution_convert_fusion.1) | copy-start | bytes 3145732
  190.9 2.0 copy-start.17
  193.9 2.2 copy-start.24
  194.0 2.2 copy-start.54
  194.0 6.7 %copy-start.60 = (bf16[2048,1024]{1,0:T(8,128)(2,1)S(1)}, bf16[2048,1024]{1,0:T(8,128)(2,1)}, u32[]{:S(2)}) copy-start(bf16[2048,1024]{1,0:T(8,128)(2,1)} %copy-done.59) | copy-start | bytes 12582916
  196.1 2.8 copy-start.25
  196.2 6.9 %slice-start = ((s8[8388608]{0:T(1024)(128)(4,1)}), s8[4194304]{0:T(1024)(128)(4,1)S(1)}, s32[]{:S(2)}) async-start(s8[8388608]{0:T(1024)(128)(4,1)} %bitcast.125), calls=%async_computation.1 | async-start | bytes 8388608
  197.6 1.9 copy-start.16
  199.5 3.6 slice-start.1
  200.7 2.3 copy-start.28
  207.4 1.8 copy-start.23
  207.4 1.8 copy-start.32
  209.9 1.8 copy-start.14
  214.3 2.4 copy-start.19
  217.6 3.0 copy-start.55
  217.6 144.7 %copy-start.40 = (f32[8,32,32]{2,1,0:T(8,128)S(1)}, f32[8,32,32]{2,1,0:T(8,128)}, u32[]{:S(2)}) copy-start(f32[8,32,32]{2,1,0:T(8,128)} %copy-done.39) | copy-start | bytes 98308
  217.6 145.8 %copy-start.36 = (f32[8,32,32]{2,1,0:T(8,128)S(1)}, f32[8,32,32]{2,1,0:T(8,128)}, u32[]{:S(2)}) copy-start(f32[8,32,32]{2,1,0:T(8,128)} %copy-done.35) | copy-start | bytes 98308
  (16 other events, 18.2 us)
Sparse Core Ops, SparseCore 0:
  207.5 150.1 all-reduce.4
